TPU v7x, 256 devices: a whole 4x4x8 slice. The times are simulated.
256 devices in a mesh: dp: 16 (over z_lo, x), tensor: 16 (over y, z_hi, core).
Axes of the slice: x: 4, y: 4, z: 8 (z_hi: 2, z_lo: 4; z = z_hi * 4 + z_lo), core: 2. Of those that a mesh axis runs over, the one named last changes fastest.
Arguments:
- out_grad: bfloat16 [2048, 5120], P('dp'), may hold values from -6 to 6
- gate_act: bfloat16 [2048, 25600], P('dp', 'tensor'), may hold values from -6 to 6
- up_act: bfloat16 [2048, 25600], P('dp', 'tensor'), may hold values from -6 to 6
- codes: int32 [5120, 25600], P('dp', 'tensor'), may hold values from 0 to 15
- zero_points: int32 [5120, 400], P('dp', 'tensor'), may hold values from 0 to 15
- scales: float32 [5120, 400], P('dp', 'tensor'), may hold values from 0.0009782797 to 0.003913119
- rotation: bfloat16 [1600, 1600], replicated, may hold values from -0.15625 to 0.15625
Outputs:
- grad_gate: bfloat16 [2048, 25600], P('dp', 'tensor')
- grad_up: bfloat16 [2048, 25600], P('dp', 'tensor')
- log_scale_grad: float32 [5120, 400], P('dp', 'tensor')
All inputs are finite; a program needn't handle non-finite values.
Results may differ from a plain program's by a relative error of at most 0.011.
Values may be sent and summed in bfloat16 or wider, within the bound.
A program may use at most 128 MiB of HBM per device.

v0:
```python
import math
import jax
import jax.numpy as jnp
from jax import lax
from jax.sharding import PartitionSpec as P


def sylvester(order_size):
    indices = jnp.arange(order_size, dtype=jnp.int32)
    common_bits = indices[:, None] & indices[None, :]
    parity = jnp.zeros((order_size, order_size), jnp.int32)
    for bit_number in range(order_size.bit_length()):
        parity = parity + (common_bits >> bit_number & 1)
    return (1 - 2 * (parity % 2)).astype(jnp.float32)


def spread(blocks, block_size):
    tok_rows = blocks.shape[0]
    local_blocks = blocks.shape[1] // block_size
    devices = lax.axis_size("tensor")
    norm_factor = 1.0 / math.sqrt(devices * local_blocks)
    hadamard = sylvester(devices * local_blocks).reshape(
        devices, local_blocks, devices, local_blocks
    )
    stacked = blocks.reshape(1, tok_rows, local_blocks, block_size)
    summed = jnp.einsum(
        "qtjc,qjpk->ptkc",
        lax.all_to_all(stacked, "tensor", split_axis=3, concat_axis=0, tiled=True).astype(
            jnp.float32
        ),
        hadamard,
        precision=lax.Precision.HIGHEST,
    )
    summed = (summed * norm_factor).astype(jnp.bfloat16)
    result = lax.all_to_all(summed, "tensor", split_axis=0, concat_axis=3, tiled=True)
    return result.reshape(tok_rows, local_blocks * block_size)


def on_device(out_grad, gate_act, up_act, codes, zero_points, scales, rotation):
    columns = gate_act.shape[1]
    block_size = rotation.shape[0]
    feat_rows = codes.shape[0]
    groups_here = scales.shape[1]
    group_cols = columns // groups_here
    gate32 = gate_act.astype(jnp.float32)
    up32 = up_act.astype(jnp.float32)
    sigmoid_gate = jax.nn.sigmoid(gate32)
    hidden = (gate32 * sigmoid_gate * up32).astype(jnp.bfloat16)
    mixed = jnp.dot(hidden, rotation, preferred_element_type=jnp.float32)
    mixed = mixed.astype(jnp.bfloat16)
    rotated = spread(mixed, block_size)
    levels = (codes.reshape(feat_rows, groups_here, group_cols) - zero_points[:, :, None]).astype(
        jnp.float32
    )
    weight = (levels * scales[:, :, None]).astype(jnp.bfloat16).reshape(feat_rows, columns)
    grad_slice = lax.all_to_all(out_grad, "dp", split_axis=1, concat_axis=0, tiled=True)
    weight_grad = lax.dot_general(
        grad_slice,
        lax.all_gather(rotated, "dp", axis=0, tiled=True),
        (((0,), (0,)), ((), ())),
        preferred_element_type=jnp.float32,
    )
    log_scale_grad = (
        jnp.sum(weight_grad.reshape(feat_rows, groups_here, group_cols) * levels, axis=2) * scales
    )
    grad_rotated = lax.psum_scatter(
        jnp.dot(grad_slice, weight, preferred_element_type=jnp.float32),
        "dp",
        scatter_dimension=0,
        tiled=True,
    )
    grad_mixed = spread(grad_rotated.astype(jnp.bfloat16), block_size)
    grad_hidden = lax.dot_general(
        grad_mixed, rotation, (((1,), (1,)), ((), ())), preferred_element_type=jnp.float32
    )
    grad_gate = (grad_hidden * up32 * sigmoid_gate * (1.0 + gate32 * (1.0 - sigmoid_gate))).astype(
        jnp.bfloat16
    )
    grad_up = (grad_hidden * gate32 * sigmoid_gate).astype(jnp.bfloat16)
    return (grad_gate, grad_up, log_scale_grad)


def solution(mesh):
    return jax.shard_map(
        on_device,
        mesh=mesh,
        in_specs=(
            P("dp", None),
            P("dp", "tensor"),
            P("dp", "tensor"),
            P("dp", "tensor"),
            P("dp", "tensor"),
            P("dp", "tensor"),
            P(),
        ),
        out_specs=(P("dp", "tensor"), P("dp", "tensor"), P("dp", "tensor")),
        check_vma=False,
    )
```

profile of v0, /device:TPU:90, one launch (start us, length us, event | category | flops | bytes accessed | tf_op | source)
XLA Modules:
  0.0 396.5 jit_solution(10725968039748546528)
XLA Ops:
  7.2 2.4 copy.24
  9.6 8.0 %all-to-all-start = ((bf16[128,16,320]{0,2,1:T(8,128)(2,1)}), bf16[128,16,320]{0,2,1:T(8,128)(2,1)}, u32[]{:S(2)}, u32[]{:S(2)}) async-start(bf16[128,16,320]{0,2,1:T(8,128)(2,1)} %bitcast.4), calls=%async_computation | async-start | bytes 2621440 | tf_op jit(solution)/shard_map/all_to_all | solution.py:56
  17.6 0.0 copy-start.1
  17.6 0.0 reduce-scatter.2.cloned.1.call-start
  17.7 2.4 copy.23
  20.0 0.0 copy-done
  20.1 0.0 copy-done.1
  20.1 1.3 fusion
  21.4 26.8 %all-to-all-done = bf16[128,16,320]{0,2,1:T(8,128)(2,1)} async-done(((bf16[128,16,320]{0,2,1:T(8,128)(2,1)}), bf16[128,16,320]{0,2,1:T(8,128)(2,1)}, u32[]{:S(2)}, u32[]{:S(2)}) %all-to-all-start) | async-done | bytes 1310752 | tf_op jit(solution)/shard_map/all_to_all | solution.py:56
  48.2 9.9 %convolution_bitcast_fusion = f32[2048,1600]{0,1:T(8,128)} fusion(bf16[320,1600]{0,1:T(8,128)(2,1)} %fusion, bf16[128,16,320]{0,2,1:T(8,128)(2,1)} %all-to-all-done), kind=kOutput, calls=%fused_computation | convolution fusion | flops 2097152000 | bytes 15441920 | tf_op jit(solution)/shard_map/dot_general | solution.py:67
  58.1 0.0 reduce-scatter.2.cloned.1.call-update
  58.1 0.5 all-gather.2.cloned.1.call-start
  58.6 0.5 copy-done.2
  59.1 0.1 copy-done.3
  59.2 4.7 %fusion.2 = bf16[1,128,1,1600]{1,3,2,0:T(8,128)(2,1)S(1)} fusion(bf16[1600,1600]{1,0:T(8,128)(2,1)} %param.13, bf16[128,1600]{0,1:T(8,128)(2,1)S(1)} %copy-done.3, bf16[128,1600]{0,1:T(8,128)(2,1)S(1)} %copy-done.2), kind=kOutput, calls=%fused_computation.8 | convolution fusion | flops 657203200 | bytes 6348800 | tf_op jit(solution)/shard_map/dot_general | solution.py:49
  63.9 6.4 %copy.55 = bf16[1,128,1,1600]{1,2,0,3:T(2,128)(2,1)S(1)} copy(bf16[1,128,1,1600]{1,3,2,0:T(8,128)(2,1)S(1)} %fusion.2) | data formatting | bytes 819200 | tf_op jit(solution)/shard_map/reshape | solution.py:25
  70.3 0.5 broadcast.409
  70.8 9.9 %reduce.5 = bf16[1600,128]{1,0:T(8,128)(2,1)} reduce(bf16[1600,1,1,128]{3,2,1,0:T(2,128)(2,1)S(1)} %bitcast.84, bf16[]{:T(256)} %broadcast.409), dimensions={1,2}, to_apply=%bitcast.80.reduce_sub_computation | reduce | bytes 819202
  80.7 1.1 reshape.191
  81.8 21.4 %all_to_all.79 = bf16[16,2,6400]{2,1,0:T(2,128)(2,1)} all-to-all(bf16[16,2,6400]{2,1,0:T(2,128)(2,1)S(1)} %reshape.191), channel_id=1, replica_groups=mesh['dp'=16,'tensor'=16] {'tensor'}, dimensions={0} | all-to-all | bytes 819200 | tf_op jit(solution)/shard_map/all_to_all | solution.py:28
  103.2 2.7 reshape.192
  106.0 7.6 %bitcast_reduce_fusion = bf16[128,1600]{0,1:T(8,128)(2,1)} fusion(bf16[1600,1,1,128]{3,2,1,0:T(2,128)(2,1)S(1)} %reshape.192), kind=kLoop, calls=%fused_computation.60 | loop fusion | bytes 819200 | tf_op jit(solution)/shard_map/all_to_all | solution.py:28
  113.6 1.1 all_to_all.69
  114.6 0.5 fusion.7
  115.1 0.1 copy.31
  115.3 18.8 %all_to_all.80 = bf16[16,128,1,100]{1,3,2,0:T(8,128)(2,1)S(1)} all-to-all(bf16[16,128,1,100]{1,3,2,0:T(8,128)(2,1)S(1)} %copy.31), channel_id=1, replica_groups=mesh['dp'=16,'tensor'=16] {'tensor'}, dimensions={0} | all-to-all | bytes 819200 | tf_op jit(solution)/shard_map/all_to_all | solution.py:35
  134.1 0.8 reshape.183
  134.9 0.0 all-gather.2.cloned.1.call-update
  134.9 83.6 %reduce-scatter.2.cloned.1.call-done = f32[128,1600]{0,1:T(8,128)} async-done(((f32[2048,1600]{0,1:T(8,128)}), f32[128,1600]{0,1:T(8,128)}) %reduce-scatter.2.cloned.1.call-update) | async-done | bytes 819216 | tf_op jit(solution)/shard_map/reduce_scatter | solution.py:66
  218.6 1.2 convert_bitcast_fusion
  219.8 6.4 %copy.56 = bf16[1,128,1,1600]{1,2,0,3:T(2,128)(2,1)S(1)} copy(bf16[1,128,1,1600]{1,3,2,0:T(8,128)(2,1)S(1)} %convert_bitcast_fusion) | data formatting | bytes 819200 | tf_op jit(solution)/shard_map/reshape | solution.py:25
  226.1 9.9 %reduce.4 = bf16[1600,128]{1,0:T(8,128)(2,1)} reduce(bf16[1600,1,1,128]{3,2,1,0:T(2,128)(2,1)S(1)} %bitcast.85, bf16[]{:T(256)} %broadcast.409), dimensions={1,2}, to_apply=%bitcast.81.reduce_sub_computation | reduce | bytes 819202
  236.0 1.1 reshape.189
  237.1 20.5 %all_to_all.81 = bf16[16,2,6400]{2,1,0:T(2,128)(2,1)} all-to-all(bf16[16,2,6400]{2,1,0:T(2,128)(2,1)S(1)} %reshape.189), channel_id=1, replica_groups=mesh['dp'=16,'tensor'=16] {'tensor'}, dimensions={0} | all-to-all | bytes 819200 | tf_op jit(solution)/shard_map/all_to_all | solution.py:28
  257.7 2.7 reshape.190
  260.4 7.6 %bitcast_reduce_fusion.1 = bf16[128,1600]{0,1:T(8,128)(2,1)} fusion(bf16[1600,1,1,128]{3,2,1,0:T(2,128)(2,1)S(1)} %reshape.190), kind=kLoop, calls=%fused_computation.61 | loop fusion | bytes 819200 | tf_op jit(solution)/shard_map/all_to_all | solution.py:28
  268.0 1.1 all_to_all.63
  269.1 0.5 fusion.8
  269.6 0.9 copy.28
  270.5 5.8 %all-to-all-start.2 = ((bf16[16,128,1,100]{1,3,2,0:T(8,128)(2,1)}), bf16[16,128,1,100]{1,3,2,0:T(8,128)(2,1)S(1)}, u32[]{:S(2)}, u32[]{:S(2)}) async-start(bf16[16,128,1,100]{1,3,2,0:T(8,128)(2,1)} %copy.28), calls=%async_computation.3 | async-start | bytes 851968 | tf_op jit(solution)/shard_map/all_to_all | solution.py:35
  276.3 94.5 %all-gather.2.cloned.1.call-done = bf16[2048,1600]{0,1:T(8,128)(2,1)} async-done(((bf16[128,1600]{0,1:T(8,128)(2,1)}), bf16[2048,1600]{0,1:T(8,128)(2,1)}) %all-gather.2.cloned.1.call-update) | async-done | bytes 6553616 | tf_op jit(solution)/shard_map/all_gather | solution.py:59
  370.8 7.1 %convolution_bitcast_fusion.1 = f32[320,1600]{1,0:T(8,128)} fusion(bf16[2048,1600]{0,1:T(8,128)(2,1)} %all-gather.2.cloned.1.call-done, bf16[128,16,320]{0,2,1:T(8,128)(2,1)} %all-to-all-done), kind=kOutput, calls=%fused_computation.1 | convolution fusion | flops 2097152000 | bytes 9912320 | tf_op jit(solution)/shard_map/dot_general | solution.py:57
  377.9 3.1 copy.32
  381.0 2.3 multiply_reduce_fusion
  383.3 0.6 mul.90
  384.0 0.0 all-to-all-done.2
  384.0 0.1 reshape.180
  384.0 5.3 %fusion.20 = (bf16[128,1600]{0,1:T(8,128)(2,1)}, bf16[128,1600]{0,1:T(8,128)(2,1)}) fusion(bf16[128,1600]{0,1:T(8,128)(2,1)} %param.8, bf16[128,1600]{0,1:T(8,128)(2,1)} %param.9, bf16[1600,1600]{1,0:T(8,128)(2,1)} %param.13, bf16[128,1600]{0,1:T(8,128)(2,1)S(1)} %reshape.180), kind=kOutput, calls=%fused_computation.34 | convolution fusion | flops 658432000 | bytes 7168000 | tf_op jit(solution)/shard_map/dot_general | solution.py:73
  (3 shorter events, 0.0 us)
Async XLA Ops:
  9.6 38.6 %all-to-all-start = ((bf16[128,16,320]{0,2,1:T(8,128)(2,1)}), bf16[128,16,320]{0,2,1:T(8,128)(2,1)}, u32[]{:S(2)}, u32[]{:S(2)}) async-start(bf16[128,16,320]{0,2,1:T(8,128)(2,1)} %bitcast.4), calls=%async_computation | async-start | bytes 2621440 | tf_op jit(solution)/shard_map/all_to_all | solution.py:56
  17.6 2.4 copy-start
  17.6 2.4 copy-start.1
  17.6 200.9 %reduce-scatter.2.cloned.1.call-start = ((), (), s32[]{:S(2)}) async-start(), calls=%async_computation.6 | async-start | bytes 13926400 | tf_op jit(solution)/shard_map/reduce_scatter | solution.py:66
  58.1 1.0 copy-start.2
  58.1 1.1 copy-start.3
  58.1 312.7 %all-gather.2.cloned.1.call-start = ((), (), s32[]{:S(2)}) async-start(), calls=%async_computation.7 | async-start | bytes 6963200 | tf_op jit(solution)/shard_map/all_gather | solution.py:59
  270.5 113.5 %all-to-all-start.2 = ((bf16[16,128,1,100]{1,3,2,0:T(8,128)(2,1)}), bf16[16,128,1,100]{1,3,2,0:T(8,128)(2,1)S(1)}, u32[]{:S(2)}, u32[]{:S(2)}) async-start(bf16[16,128,1,100]{1,3,2,0:T(8,128)(2,1)} %copy.28), calls=%async_computation.3 | async-start | bytes 851968 | tf_op jit(solution)/shard_map/all_to_all | solution.py:35
Sparse Core Ops, SparseCore 0:
  58.3 160.2 reduce-scatter.1
  220.9 149.8 all-gather.1
where the time goes:
time: 401 us; the launch traced here: 396 us
  waiting for transfers between devices  205 us (51%)
  blocking collectives  60.8 us (15%)
  local copies, waits for them, and re-layouts  48.7 us (12%)
  matrix products  28 us (7%)
  other arithmetic  25.3 us (6%)
  starting transfers between devices  14.4 us (4%)
  between operations  14.4 us (4%)
    all_gather x1, waiting for transfers between devices, on_device(): lax.all_gather(rotated, 'dp', axis=0, tiled=True)  94.5 us
    reduce_scatter x1, waiting for transfers between devices, on_device(): lax.psum_scatter(jnp.dot(grad_slice, weight, preferred_element_type=jnp.f...  83.6 us
    all_to_all x2, blocking collectives, spread(): lax.all_to_all(stacked, 'tensor', split_axis=3, concat_axis=0, tiled=True)  41.9 us
    all_to_all x1, waiting for transfers between devices, on_device(): lax.all_to_all(out_grad, 'dp', split_axis=1, concat_axis=0, tiled=True)  26.8 us
    unnamed x2, other arithmetic  19.8 us
    all_to_all x1, blocking collectives, spread(): lax.all_to_all(summed, 'tensor', split_axis=0, concat_axis=3, tiled=True)  18.8 us
    all_to_all x4, local copies, waits for them, and re-layouts, spread(): lax.all_to_all(stacked, 'tensor', split_axis=3, concat_axis=0, tiled=True)  17.3 us
    unnamed x15, local copies, waits for them, and re-layouts  13.6 us
  transfers between devices with their start and end apart: 4, of which 3 were waited for; matrix products, arithmetic and copies ran while one was open for 21% of the time, Pallas kernels for 0%

commit v1 on v0

--- a/solution.py
+++ b/solution.py
@@ -25,9 +25,12 @@
     stacked = blocks.reshape(1, tok_rows, local_blocks, block_size)
     summed = jnp.einsum(
         "qtjc,qjpk->ptkc",
-        lax.all_to_all(stacked, "tensor", split_axis=3, concat_axis=0, tiled=True).astype(
-            jnp.float32
-        ),
+        jnp.concatenate(
+            lax.all_to_all(
+                jnp.stack(jnp.split(stacked, lax.axis_size("tensor"), axis=3)), "tensor", 0, 0
+            ),
+            axis=0,
+        ).astype(jnp.float32),
         hadamard,
         precision=lax.Precision.HIGHEST,
     )

time: 401 us -> 388 us (0.968)
  waiting for transfers between devices: 205 us -> 249 us
  local copies, waits for them, and re-layouts: 48.7 us -> 11.4 us
  other arithmetic: 25.3 us -> 5.46 us
    reduce_scatter x1, waiting for transfers between devices: 83.6 us -> 113 us  [on_device(): lax.psum_scatter(jnp.dot(grad_slice, weight, preferred_element_type=jnp.f...]
    unnamed x2 -> x0, other arithmetic: 19.8 us -> none
    all_to_all x4 -> x0, local copies, waits for them, and re-layouts: 17.3 us -> none  [spread(): lax.all_to_all(stacked, 'tensor', split_axis=3, concat_axis=0, tiled=True)]
    all_gather x1, waiting for transfers between devices: 94.5 us -> 110 us  [on_device(): lax.all_gather(rotated, 'dp', axis=0, tiled=True)]
    reshape x2 -> x0, local copies, waits for them, and re-layouts: 12.7 us -> none  [spread(): stacked = blocks.reshape(1, tok_rows, local_blocks, block_size)]
    unnamed x15 -> x40, local copies, waits for them, and re-layouts: 13.6 us -> 6.28 us
  transfers between devices with their start and end apart: 4 -> 4, of which waited for: 3 -> 3; matrix products, arithmetic and copies ran while one was open for 21% -> 7% of each run, Pallas kernels for 0% -> 0%
where the time goes in v1:
time: 388 us; the launch traced here: 383 us
  waiting for transfers between devices  249 us (64%)
  blocking collectives  60.6 us (16%)
  matrix products  27.9 us (7%)
  between operations  14.3 us (4%)
  starting transfers between devices  13.9 us (4%)
  local copies, waits for them, and re-layouts  11.4 us (3%)
  other arithmetic  5.46 us (1%)
    reduce_scatter x1, waiting for transfers between devices, on_device(): lax.psum_scatter(jnp.dot(grad_slice, weight, preferred_element_type=jnp.f...  113 us
    all_gather x1, waiting for transfers between devices, on_device(): lax.all_gather(rotated, 'dp', axis=0, tiled=True)  110 us
    all_to_all x2, blocking collectives, spread(): lax.all_to_all(jnp.stack(jnp.split(stacked, lax.axis_size('tensor'), axis...  41.8 us
    all_to_all x1, waiting for transfers between devices, on_device(): lax.all_to_all(out_grad, 'dp', split_axis=1, concat_axis=0, tiled=True)  26.8 us
    all_to_all x1, blocking collectives, spread(): lax.all_to_all(summed, 'tensor', split_axis=0, concat_axis=3, tiled=True)  18.8 us
    dot_general x1, matrix products, on_device(): jnp.dot(grad_slice, weight, preferred_element_type=jnp.float32)  9.93 us
    all_to_all x1, starting transfers between devices, on_device(): lax.all_to_all(out_grad, 'dp', split_axis=1, concat_axis=0, tiled=True)  8 us
  transfers between devices with their start and end apart: 4, of which 3 were waited for; matrix products, arithmetic and copies ran while one was open for 7% of the time, Pallas kernels for 0%

profile of v1, /device:TPU:90, one launch (start us, length us, event | category | flops | bytes accessed | tf_op | source)
XLA Modules:
  0.0 382.9 jit_solution(16542730054971142537)
XLA Ops:
  7.2 2.4 copy.24
  9.6 8.0 %all-to-all-start = ((bf16[128,16,320]{0,2,1:T(8,128)(2,1)}), bf16[128,16,320]{0,2,1:T(8,128)(2,1)}, u32[]{:S(2)}, u32[]{:S(2)}) async-start(bf16[128,16,320]{0,2,1:T(8,128)(2,1)} %bitcast.4), calls=%async_computation | async-start | bytes 2621440 | tf_op jit(solution)/shard_map/all_to_all | solution.py:59
  17.6 0.0 copy-start
  17.6 0.0 copy-start.1
  17.6 0.0 reduce-scatter.2.cloned.1.call-start
  17.7 2.4 copy.23
  20.0 0.0 copy-done
  20.1 0.0 copy-done.1
  20.1 1.3 fusion
  21.4 26.8 %all-to-all-done = bf16[128,16,320]{0,2,1:T(8,128)(2,1)} async-done(((bf16[128,16,320]{0,2,1:T(8,128)(2,1)}), bf16[128,16,320]{0,2,1:T(8,128)(2,1)}, u32[]{:S(2)}, u32[]{:S(2)}) %all-to-all-start) | async-done | bytes 1310752 | tf_op jit(solution)/shard_map/all_to_all | solution.py:59
  48.2 9.9 %convolution_bitcast_fusion = f32[2048,1600]{0,1:T(8,128)} fusion(bf16[320,1600]{0,1:T(8,128)(2,1)} %fusion, bf16[128,16,320]{0,2,1:T(8,128)(2,1)} %all-to-all-done), kind=kOutput, calls=%fused_computation | convolution fusion | flops 2097152000 | bytes 15441920 | tf_op jit(solution)/shard_map/dot_general | solution.py:70
  58.1 0.0 copy-start.2
  58.1 0.0 copy-start.3
  58.1 0.0 reduce-scatter.2.cloned.1.call-update
  58.1 0.0 all-gather.2.cloned.1.call-start
  58.2 0.9 copy-done.2
  59.1 0.1 copy-done.3
  59.2 4.7 %fusion.2 = bf16[1,128,1,1600]{1,3,2,0:T(8,128)(2,1)S(1)} fusion(bf16[1600,1600]{1,0:T(8,128)(2,1)} %param.13, bf16[128,1600]{0,1:T(8,128)(2,1)S(1)} %copy-done.3, bf16[128,1600]{0,1:T(8,128)(2,1)S(1)} %copy-done.2), kind=kOutput, calls=%fused_computation.8 | convolution fusion | flops 657203200 | bytes 6348800 | tf_op jit(solution)/shard_map/dot_general | solution.py:52
  64.3 21.5 %all_to_all.59 = bf16[16,1,128,1,100]{2,4,3,1,0:T(8,128)(2,1)S(1)} all-to-all(bf16[16,1,128,1,100]{2,4,3,1,0:T(8,128)(2,1)S(1)} %constant_dynamic-update-slice_fusion.16), channel_id=1, replica_groups=mesh['dp'=16,'tensor'=16] {'tensor'}, dimensions={0} | all-to-all | bytes 819200 | tf_op jit(solution)/shard_map/all_to_all | solution.py:29
  85.7 0.5 fusion.7
  86.2 0.1 copy.29
  86.3 18.8 %all_to_all.60 = bf16[16,128,1,100]{1,3,2,0:T(8,128)(2,1)S(1)} all-to-all(bf16[16,128,1,100]{1,3,2,0:T(8,128)(2,1)S(1)} %copy.29), channel_id=1, replica_groups=mesh['dp'=16,'tensor'=16] {'tensor'}, dimensions={0} | all-to-all | bytes 819200 | tf_op jit(solution)/shard_map/all_to_all | solution.py:38
  105.1 0.8 reshape.185
  106.0 0.0 all-gather.2.cloned.1.call-update
  106.0 112.9 %reduce-scatter.2.cloned.1.call-done = f32[128,1600]{0,1:T(8,128)} async-done(((f32[2048,1600]{0,1:T(8,128)}), f32[128,1600]{0,1:T(8,128)}) %reduce-scatter.2.cloned.1.call-update) | async-done | bytes 819216 | tf_op jit(solution)/shard_map/reduce_scatter | solution.py:69
  218.9 1.2 convert_bitcast_fusion
  220.4 20.3 %all_to_all.61 = bf16[16,1,128,1,100]{2,4,3,1,0:T(8,128)(2,1)S(1)} all-to-all(bf16[16,1,128,1,100]{2,4,3,1,0:T(8,128)(2,1)S(1)} %constant_dynamic-update-slice_fusion), channel_id=1, replica_groups=mesh['dp'=16,'tensor'=16] {'tensor'}, dimensions={0} | all-to-all | bytes 819200 | tf_op jit(solution)/shard_map/all_to_all | solution.py:29
  240.7 0.5 fusion.8
  241.2 0.9 copy.27
  242.0 5.8 %all-to-all-start.2 = ((bf16[16,128,1,100]{1,3,2,0:T(8,128)(2,1)}), bf16[16,128,1,100]{1,3,2,0:T(8,128)(2,1)S(1)}, u32[]{:S(2)}, u32[]{:S(2)}) async-start(bf16[16,128,1,100]{1,3,2,0:T(8,128)(2,1)} %copy.27), calls=%async_computation.3 | async-start | bytes 851968 | tf_op jit(solution)/shard_map/all_to_all | solution.py:38
  247.8 109.7 %all-gather.2.cloned.1.call-done = bf16[2048,1600]{0,1:T(8,128)(2,1)} async-done(((bf16[128,1600]{0,1:T(8,128)(2,1)}), bf16[2048,1600]{0,1:T(8,128)(2,1)}) %all-gather.2.cloned.1.call-update) | async-done | bytes 6553616 | tf_op jit(solution)/shard_map/all_gather | solution.py:62
  357.5 7.1 %convolution_bitcast_fusion.1 = f32[320,1600]{1,0:T(8,128)} fusion(bf16[2048,1600]{0,1:T(8,128)(2,1)} %all-gather.2.cloned.1.call-done, bf16[128,16,320]{0,2,1:T(8,128)(2,1)} %all-to-all-done), kind=kOutput, calls=%fused_computation.1 | convolution fusion | flops 2097152000 | bytes 9912320 | tf_op jit(solution)/shard_map/dot_general | solution.py:60
  364.6 3.2 copy.30
  367.7 2.3 multiply_reduce_fusion
  370.1 0.6 mul.90
  370.7 0.0 all-to-all-done.2
  370.7 0.1 reshape.182
  370.8 5.2 %fusion.20 = (bf16[128,1600]{0,1:T(8,128)(2,1)}, bf16[128,1600]{0,1:T(8,128)(2,1)}) fusion(bf16[128,1600]{0,1:T(8,128)(2,1)S(1)} %copy-done.2, bf16[128,1600]{0,1:T(8,128)(2,1)} %param.9, bf16[1600,1600]{1,0:T(8,128)(2,1)} %param.13, bf16[128,1600]{0,1:T(8,128)(2,1)S(1)} %reshape.182), kind=kOutput, calls=%fused_computation.34 | convolution fusion | flops 658432000 | bytes 7168000 | tf_op jit(solution)/shard_map/dot_general | solution.py:76
  (32 shorter events, 0.5 us)
Async XLA Ops:
  9.6 38.6 %all-to-all-start = ((bf16[128,16,320]{0,2,1:T(8,128)(2,1)}), bf16[128,16,320]{0,2,1:T(8,128)(2,1)}, u32[]{:S(2)}, u32[]{:S(2)}) async-start(bf16[128,16,320]{0,2,1:T(8,128)(2,1)} %bitcast.4), calls=%async_computation | async-start | bytes 2621440 | tf_op jit(solution)/shard_map/all_to_all | solution.py:59
  17.6 2.4 copy-start
  17.6 2.4 copy-start.1
  17.6 201.2 %reduce-scatter.2.cloned.1.call-start = ((), (), s32[]{:S(2)}) async-start(), calls=%async_computation.6 | async-start | bytes 13926400 | tf_op jit(solution)/shard_map/reduce_scatter | solution.py:69
  58.1 1.0 copy-start.2
  58.1 1.1 copy-start.3
  58.1 299.4 %all-gather.2.cloned.1.call-start = ((), (), s32[]{:S(2)}) async-start(), calls=%async_computation.7 | async-start | bytes 6963200 | tf_op jit(solution)/shard_map/all_gather | solution.py:62
  242.0 128.7 %all-to-all-start.2 = ((bf16[16,128,1,100]{1,3,2,0:T(8,128)(2,1)}), bf16[16,128,1,100]{1,3,2,0:T(8,128)(2,1)S(1)}, u32[]{:S(2)}, u32[]{:S(2)}) async-start(bf16[16,128,1,100]{1,3,2,0:T(8,128)(2,1)} %copy.27), calls=%async_computation.3 | async-start | bytes 851968 | tf_op jit(solution)/shard_map/all_to_all | solution.py:38
Sparse Core Ops, SparseCore 0:
  58.3 160.5 reduce-scatter.1
  221.1 136.3 all-gather.1
